TPU v7x, 512 devices: a whole 4x4x16 slice. The times are simulated.
512 devices in a mesh: row: 16 (over z), col: 16 (over y_hi, x, core), fr: 2 (over y_lo).
Axes of the slice: x: 4, y: 4 (y_hi: 2, y_lo: 2; y = y_hi * 2 + y_lo), z: 16, core: 2. Of those that a mesh axis runs over, the one named last changes fastest.
Arguments:
- sigma_aa: float32 [12288, 12288], P(('fr', 'row'), 'col'), parts along dimension 0, may hold values from -6 to 6
- l_as: float32 [24576, 6144], P(('fr', 'row'), 'col'), parts along dimension 0, may hold values from -0.078125 to 0.078125
- block_mask: int32 [32, 16], P(('fr', 'row'), 'col'), parts along dimension 0, may hold values 0 or 1
Outputs:
- sigma_as: float32 [12288, 6144], P(('fr', 'row'), 'col'), parts along dimension 0
There are 2 independent parts, one for each index of `fr`. A program takes and returns all parts, laid end to end along the dimension named above; each array names one. Nothing has to cross between parts.
All inputs are finite; a program needn't handle non-finite values. No bound on the sum of `block_mask` on one device may be relied on, other than what follows from the above.
Results may differ from a plain program's by a relative error of at most 0.0003.
Values sent between devices are 32-bit elements; how exact they have to be, the bound alone decides.
A program may use at most 64 MiB of HBM per device.

v0:
```python
import jax
import jax.numpy as jnp
from jax import lax
from jax.sharding import PartitionSpec as P


def passed_along(block, axis, distance):
    devices = range(lax.axis_size(axis))
    route = [((i - distance) % len(devices), i) for i in devices]
    return lax.ppermute(block, axis, route)


def product(lhs_block, rhs_block):
    return jnp.dot(
        lhs_block, rhs_block, preferred_element_type=jnp.float32, precision=lax.Precision.HIGHEST
    )


def body(sigma_aa, l_as, block_mask):
    factor = l_as * block_mask.astype(jnp.float32)
    half_steps = lax.axis_size("row") // 2
    partial_value = jnp.zeros((sigma_aa.shape[0], l_as.shape[1]), jnp.float32)
    current = sigma_aa
    factor_block = factor
    for turn_index in range(half_steps):
        partial_value = partial_value + product(current, factor_block)
        if turn_index + 1 < half_steps:
            current = passed_along(current, "col", -1)
            factor_block = passed_along(factor_block, "row", -1)
    return -partial_value


def solution(mesh):
    placed = (P(("fr", "row"), "col"), P(("fr", "row"), "col"), P(("fr", "row"), "col"))
    return jax.shard_map(
        body, mesh=mesh, in_specs=placed, out_specs=P(("fr", "row"), "col"), check_vma=False
    )
```

profile of v0, /device:TPU:6, one launch (start us, length us, event | category | flops | bytes accessed | tf_op | source)
XLA Modules:
  0.0 209.4 jit_solution(8536624219745970556)
XLA Ops:
  0.7 0.0 copy-start
  0.7 1.4 broadcast_multiply_fusion
  2.1 11.4 %collective-permute-start = (f32[768,384]{1,0:T(8,128)S(1)}, f32[768,384]{1,0:T(8,128)S(1)}, u32[]{:S(2)}, u32[]{:S(2)}) collective-permute-start(f32[768,384]{1,0:T(8,128)S(1)} %broadcast_multiply_fusion), channel_id=1, source_target_pairs={{32,0},{64,32},{96,64},{128,96},{160,128},{192,160},{224,192},{256... | collective-permute-start | bytes 3538952 | tf_op jit(solution)/shard_map/ppermute | solution.py:10
  13.5 0.0 copy-done
  13.5 1.9 collective-permute-start.1
  15.5 23.3 %collective-permute-done = f32[768,384]{1,0:T(8,128)S(1)} collective-permute-done((f32[768,384]{1,0:T(8,128)S(1)}, f32[768,384]{1,0:T(8,128)S(1)}, u32[]{:S(2)}, u32[]{:S(2)}) %collective-permute-start) | collective-permute-done | bytes 1179680 | tf_op jit(solution)/shard_map/ppermute | solution.py:10
  38.7 5.6 %collective-permute-start.2 = (f32[768,384]{1,0:T(8,128)S(1)}, f32[768,384]{1,0:T(8,128)S(1)}, u32[]{:S(2)}, u32[]{:S(2)}) collective-permute-start(f32[768,384]{1,0:T(8,128)S(1)} %collective-permute-done), channel_id=1, source_target_pairs={{32,0},{64,32},{96,64},{128,96},{160,128},{192,160},{224,192},{256... | collective-permute-start | bytes 3538952 | tf_op jit(solution)/shard_map/ppermute | solution.py:10
  44.3 0.0 collective-permute-done.1
  44.3 1.9 collective-permute-start.3
  46.3 22.4 %collective-permute-done.2 = f32[768,384]{1,0:T(8,128)S(1)} collective-permute-done((f32[768,384]{1,0:T(8,128)S(1)}, f32[768,384]{1,0:T(8,128)S(1)}, u32[]{:S(2)}, u32[]{:S(2)}) %collective-permute-start.2) | collective-permute-done | bytes 1179680 | tf_op jit(solution)/shard_map/ppermute | solution.py:10
  68.7 5.6 %collective-permute-start.4 = (f32[768,384]{1,0:T(8,128)S(1)}, f32[768,384]{1,0:T(8,128)S(1)}, u32[]{:S(2)}, u32[]{:S(2)}) collective-permute-start(f32[768,384]{1,0:T(8,128)S(1)} %collective-permute-done.2), channel_id=1, source_target_pairs={{32,0},{64,32},{96,64},{128,96},{160,128},{192,160},{224,192},{256... | collective-permute-start | bytes 3538952 | tf_op jit(solution)/shard_map/ppermute | solution.py:10
  74.3 0.0 collective-permute-done.3
  74.3 1.9 collective-permute-start.5
  76.2 21.5 %collective-permute-done.4 = f32[768,384]{1,0:T(8,128)S(1)} collective-permute-done((f32[768,384]{1,0:T(8,128)S(1)}, f32[768,384]{1,0:T(8,128)S(1)}, u32[]{:S(2)}, u32[]{:S(2)}) %collective-permute-start.4) | collective-permute-done | bytes 1179680 | tf_op jit(solution)/shard_map/ppermute | solution.py:10
  97.7 5.6 %collective-permute-start.6 = (f32[768,384]{1,0:T(8,128)S(1)}, f32[768,384]{1,0:T(8,128)S(1)}, u32[]{:S(2)}, u32[]{:S(2)}) collective-permute-start(f32[768,384]{1,0:T(8,128)S(1)} %collective-permute-done.4), channel_id=1, source_target_pairs={{32,0},{64,32},{96,64},{128,96},{160,128},{192,160},{224,192},{256... | collective-permute-start | bytes 3538952 | tf_op jit(solution)/shard_map/ppermute | solution.py:10
  103.3 0.0 collective-permute-done.5
  103.3 1.9 collective-permute-start.7
  105.2 20.6 %collective-permute-done.6 = f32[768,384]{1,0:T(8,128)S(1)} collective-permute-done((f32[768,384]{1,0:T(8,128)S(1)}, f32[768,384]{1,0:T(8,128)S(1)}, u32[]{:S(2)}, u32[]{:S(2)}) %collective-permute-start.6) | collective-permute-done | bytes 1179680 | tf_op jit(solution)/shard_map/ppermute | solution.py:10
  125.7 5.6 %collective-permute-start.8 = (f32[768,384]{1,0:T(8,128)S(1)}, f32[768,384]{1,0:T(8,128)S(1)}, u32[]{:S(2)}, u32[]{:S(2)}) collective-permute-start(f32[768,384]{1,0:T(8,128)S(1)} %collective-permute-done.6), channel_id=1, source_target_pairs={{32,0},{64,32},{96,64},{128,96},{160,128},{192,160},{224,192},{256... | collective-permute-start | bytes 3538952 | tf_op jit(solution)/shard_map/ppermute | solution.py:10
  131.3 0.0 collective-permute-done.7
  131.4 1.9 collective-permute-start.9
  133.3 19.6 %collective-permute-done.8 = f32[768,384]{1,0:T(8,128)S(1)} collective-permute-done((f32[768,384]{1,0:T(8,128)S(1)}, f32[768,384]{1,0:T(8,128)S(1)}, u32[]{:S(2)}, u32[]{:S(2)}) %collective-permute-start.8) | collective-permute-done | bytes 1179680 | tf_op jit(solution)/shard_map/ppermute | solution.py:10
  152.9 5.6 %collective-permute-start.10 = (f32[768,384]{1,0:T(8,128)S(1)}, f32[768,384]{1,0:T(8,128)S(1)}, u32[]{:S(2)}, u32[]{:S(2)}) collective-permute-start(f32[768,384]{1,0:T(8,128)S(1)} %collective-permute-done.8), channel_id=1, source_target_pairs={{32,0},{64,32},{96,64},{128,96},{160,128},{192,160},{224,192},{256... | collective-permute-start | bytes 3538952 | tf_op jit(solution)/shard_map/ppermute | solution.py:10
  158.5 0.0 collective-permute-done.9
  158.5 2.1 %collective-permute-start.11 = (f32[384,768]{1,0:T(8,128)S(1)}, f32[384,768]{1,0:T(8,128)S(1)}, u32[]{:S(2)}, u32[]{:S(2)}) collective-permute-start(f32[384,768]{1,0:T(8,128)S(1)} %collective-permute-done.9), channel_id=1, source_target_pairs={{2,0},{4,2},{6,4},{8,6},{10,8},{12,10},{14,12},{16,14},{18,16},{20... | collective-permute-start | bytes 3538952 | tf_op jit(solution)/shard_map/ppermute | solution.py:10
  160.6 3.8 %fusion.2 = f32[384,384]{1,0:T(8,128)S(1)} fusion(f32[768,384]{1,0:T(8,128)S(1)} %broadcast_multiply_fusion, f32[384,768]{1,0:T(8,128)S(1)} %copy-done), kind=kOutput, calls=%fused_computation.10 | convolution fusion | flops 1358954496 | bytes 2949120 | tf_op jit(solution)/shard_map/dot_general | solution.py:14
  164.5 3.8 %convolution_add_fusion.6 = f32[384,384]{1,0:T(8,128)S(1)} fusion(f32[384,384]{1,0:T(8,128)S(1)} %fusion.2, f32[768,384]{1,0:T(8,128)S(1)} %collective-permute-done, f32[384,768]{1,0:T(8,128)S(1)} %collective-permute-done.1), kind=kOutput, calls=%fused_computation.6 | convolution fusion | flops 1359101952 | bytes 3538944 | tf_op jit(solution)/shard_map/dot_general | solution.py:14
  168.3 3.8 %convolution_add_fusion.5 = f32[384,384]{1,0:T(8,128)S(1)} fusion(f32[384,384]{1,0:T(8,128)S(1)} %convolution_add_fusion.6, f32[768,384]{1,0:T(8,128)S(1)} %collective-permute-done.2, f32[384,768]{1,0:T(8,128)S(1)} %collective-permute-done.3), kind=kOutput, calls=%fused_computation.5 | convolution fusion | flops 1359101952 | bytes 3538944 | tf_op jit(solution)/shard_map/dot_general | solution.py:14
  172.1 7.0 %collective-permute-done.10 = f32[768,384]{1,0:T(8,128)S(1)} collective-permute-done((f32[768,384]{1,0:T(8,128)S(1)}, f32[768,384]{1,0:T(8,128)S(1)}, u32[]{:S(2)}, u32[]{:S(2)}) %collective-permute-start.10) | collective-permute-done | bytes 1179680 | tf_op jit(solution)/shard_map/ppermute | solution.py:10
  179.2 5.6 %collective-permute-start.12 = (f32[768,384]{1,0:T(8,128)S(1)}, f32[768,384]{1,0:T(8,128)S(1)}, u32[]{:S(2)}, u32[]{:S(2)}) collective-permute-start(f32[768,384]{1,0:T(8,128)S(1)} %collective-permute-done.10), channel_id=1, source_target_pairs={{32,0},{64,32},{96,64},{128,96},{160,128},{192,160},{224,192},{256... | collective-permute-start | bytes 3538952 | tf_op jit(solution)/shard_map/ppermute | solution.py:10
  184.8 0.0 collective-permute-done.11
  184.8 2.1 %collective-permute-start.13 = (f32[384,768]{1,0:T(8,128)S(1)}, f32[384,768]{1,0:T(8,128)S(1)}, u32[]{:S(2)}, u32[]{:S(2)}) collective-permute-start(f32[384,768]{1,0:T(8,128)S(1)} %collective-permute-done.11), channel_id=1, source_target_pairs={{2,0},{4,2},{6,4},{8,6},{10,8},{12,10},{14,12},{16,14},{18,16},{20... | collective-permute-start | bytes 3538952 | tf_op jit(solution)/shard_map/ppermute | solution.py:10
  186.9 3.8 %convolution_add_fusion.4 = f32[384,384]{1,0:T(8,128)S(1)} fusion(f32[384,384]{1,0:T(8,128)S(1)} %convolution_add_fusion.5, f32[768,384]{1,0:T(8,128)S(1)} %collective-permute-done.4, f32[384,768]{1,0:T(8,128)S(1)} %collective-permute-done.5), kind=kOutput, calls=%fused_computation.4 | convolution fusion | flops 1359101952 | bytes 3538944 | tf_op jit(solution)/shard_map/dot_general | solution.py:14
  190.7 3.8 %convolution_add_fusion.3 = f32[384,384]{1,0:T(8,128)S(1)} fusion(f32[384,384]{1,0:T(8,128)S(1)} %convolution_add_fusion.4, f32[768,384]{1,0:T(8,128)S(1)} %collective-permute-done.6, f32[384,768]{1,0:T(8,128)S(1)} %collective-permute-done.7), kind=kOutput, calls=%fused_computation.3 | convolution fusion | flops 1359101952 | bytes 3538944 | tf_op jit(solution)/shard_map/dot_general | solution.py:14
  194.6 3.8 %convolution_add_fusion.2 = f32[384,384]{1,0:T(8,128)S(1)} fusion(f32[384,384]{1,0:T(8,128)S(1)} %convolution_add_fusion.3, f32[768,384]{1,0:T(8,128)S(1)} %collective-permute-done.8, f32[384,768]{1,0:T(8,128)S(1)} %collective-permute-done.9), kind=kOutput, calls=%fused_computation.2 | convolution fusion | flops 1359101952 | bytes 3538944 | tf_op jit(solution)/shard_map/dot_general | solution.py:14
  198.4 4.1 %convolution_add_fusion.1 = f32[384,384]{1,0:T(8,128)S(1)} fusion(f32[384,384]{1,0:T(8,128)S(1)} %convolution_add_fusion.2, f32[768,384]{1,0:T(8,128)S(1)} %collective-permute-done.10, f32[384,768]{1,0:T(8,128)S(1)} %collective-permute-done.11), kind=kOutput, calls=%fused_computation.1 | convolution fusion | flops 1359101952 | bytes 3538944 | tf_op jit(solution)/shard_map/dot_general | solution.py:14
  202.5 2.0 collective-permute-done.12
  204.5 0.0 collective-permute-done.13
  204.5 3.8 %fusion.1 = f32[384,384]{0,1:T(8,128)S(1)} fusion(f32[384,384]{1,0:T(8,128)S(1)} %convolution_add_fusion.1, f32[768,384]{1,0:T(8,128)S(1)} %collective-permute-done.12, f32[384,768]{1,0:T(8,128)S(1)} %collective-permute-done.13), kind=kOutput, calls=%fused_computation.8 | convolution fusion | flops 1359249408 | bytes 3538944 | tf_op jit(solution)/shard_map/dot_general | solution.py:14
  208.3 1.1 copy.4
Async XLA Ops:
  0.7 12.9 %copy-start = (f32[384,768]{1,0:T(8,128)S(1)}, f32[384,768]{1,0:T(8,128)}, u32[]{:S(2)}) copy-start(f32[384,768]{1,0:T(8,128)} %param.3) | copy-start | bytes 3538948
  2.1 36.6 %collective-permute-start = (f32[768,384]{1,0:T(8,128)S(1)}, f32[768,384]{1,0:T(8,128)S(1)}, u32[]{:S(2)}, u32[]{:S(2)}) collective-permute-start(f32[768,384]{1,0:T(8,128)S(1)} %broadcast_multiply_fusion), channel_id=1, source_target_pairs={{32,0},{64,32},{96,64},{128,96},{160,128},{192,160},{224,192},{256... | collective-permute-start | bytes 3538952 | tf_op jit(solution)/shard_map/ppermute | solution.py:10
  13.5 30.8 %collective-permute-start.1 = (f32[384,768]{1,0:T(8,128)S(1)}, f32[384,768]{1,0:T(8,128)S(1)}, u32[]{:S(2)}, u32[]{:S(2)}) collective-permute-start(f32[384,768]{1,0:T(8,128)S(1)} %copy-done), channel_id=1, source_target_pairs={{2,0},{4,2},{6,4},{8,6},{10,8},{12,10},{14,12},{16,14},{18,16},{20... | collective-permute-start | bytes 3538952 | tf_op jit(solution)/shard_map/ppermute | solution.py:10
  38.7 29.9 %collective-permute-start.2 = (f32[768,384]{1,0:T(8,128)S(1)}, f32[768,384]{1,0:T(8,128)S(1)}, u32[]{:S(2)}, u32[]{:S(2)}) collective-permute-start(f32[768,384]{1,0:T(8,128)S(1)} %collective-permute-done), channel_id=1, source_target_pairs={{32,0},{64,32},{96,64},{128,96},{160,128},{192,160},{224,192},{256... | collective-permute-start | bytes 3538952 | tf_op jit(solution)/shard_map/ppermute | solution.py:10
  44.3 29.9 %collective-permute-start.3 = (f32[384,768]{1,0:T(8,128)S(1)}, f32[384,768]{1,0:T(8,128)S(1)}, u32[]{:S(2)}, u32[]{:S(2)}) collective-permute-start(f32[384,768]{1,0:T(8,128)S(1)} %collective-permute-done.1), channel_id=1, source_target_pairs={{2,0},{4,2},{6,4},{8,6},{10,8},{12,10},{14,12},{16,14},{18,16},{20... | collective-permute-start | bytes 3538952 | tf_op jit(solution)/shard_map/ppermute | solution.py:10
  68.7 29.0 %collective-permute-start.4 = (f32[768,384]{1,0:T(8,128)S(1)}, f32[768,384]{1,0:T(8,128)S(1)}, u32[]{:S(2)}, u32[]{:S(2)}) collective-permute-start(f32[768,384]{1,0:T(8,128)S(1)} %collective-permute-done.2), channel_id=1, source_target_pairs={{32,0},{64,32},{96,64},{128,96},{160,128},{192,160},{224,192},{256... | collective-permute-start | bytes 3538952 | tf_op jit(solution)/shard_map/ppermute | solution.py:10
  74.3 29.0 %collective-permute-start.5 = (f32[384,768]{1,0:T(8,128)S(1)}, f32[384,768]{1,0:T(8,128)S(1)}, u32[]{:S(2)}, u32[]{:S(2)}) collective-permute-start(f32[384,768]{1,0:T(8,128)S(1)} %collective-permute-done.3), channel_id=1, source_target_pairs={{2,0},{4,2},{6,4},{8,6},{10,8},{12,10},{14,12},{16,14},{18,16},{20... | collective-permute-start | bytes 3538952 | tf_op jit(solution)/shard_map/ppermute | solution.py:10
  97.7 28.1 %collective-permute-start.6 = (f32[768,384]{1,0:T(8,128)S(1)}, f32[768,384]{1,0:T(8,128)S(1)}, u32[]{:S(2)}, u32[]{:S(2)}) collective-permute-start(f32[768,384]{1,0:T(8,128)S(1)} %collective-permute-done.4), channel_id=1, source_target_pairs={{32,0},{64,32},{96,64},{128,96},{160,128},{192,160},{224,192},{256... | collective-permute-start | bytes 3538952 | tf_op jit(solution)/shard_map/ppermute | solution.py:10
  103.3 28.1 %collective-permute-start.7 = (f32[384,768]{1,0:T(8,128)S(1)}, f32[384,768]{1,0:T(8,128)S(1)}, u32[]{:S(2)}, u32[]{:S(2)}) collective-permute-start(f32[384,768]{1,0:T(8,128)S(1)} %collective-permute-done.5), channel_id=1, source_target_pairs={{2,0},{4,2},{6,4},{8,6},{10,8},{12,10},{14,12},{16,14},{18,16},{20... | collective-permute-start | bytes 3538952 | tf_op jit(solution)/shard_map/ppermute | solution.py:10
  125.7 27.2 %collective-permute-start.8 = (f32[768,384]{1,0:T(8,128)S(1)}, f32[768,384]{1,0:T(8,128)S(1)}, u32[]{:S(2)}, u32[]{:S(2)}) collective-permute-start(f32[768,384]{1,0:T(8,128)S(1)} %collective-permute-done.6), channel_id=1, source_target_pairs={{32,0},{64,32},{96,64},{128,96},{160,128},{192,160},{224,192},{256... | collective-permute-start | bytes 3538952 | tf_op jit(solution)/shard_map/ppermute | solution.py:10
  131.4 27.2 %collective-permute-start.9 = (f32[384,768]{1,0:T(8,128)S(1)}, f32[384,768]{1,0:T(8,128)S(1)}, u32[]{:S(2)}, u32[]{:S(2)}) collective-permute-start(f32[384,768]{1,0:T(8,128)S(1)} %collective-permute-done.7), channel_id=1, source_target_pairs={{2,0},{4,2},{6,4},{8,6},{10,8},{12,10},{14,12},{16,14},{18,16},{20... | collective-permute-start | bytes 3538952 | tf_op jit(solution)/shard_map/ppermute | solution.py:10
  152.9 26.2 %collective-permute-start.10 = (f32[768,384]{1,0:T(8,128)S(1)}, f32[768,384]{1,0:T(8,128)S(1)}, u32[]{:S(2)}, u32[]{:S(2)}) collective-permute-start(f32[768,384]{1,0:T(8,128)S(1)} %collective-permute-done.8), channel_id=1, source_target_pairs={{32,0},{64,32},{96,64},{128,96},{160,128},{192,160},{224,192},{256... | collective-permute-start | bytes 3538952 | tf_op jit(solution)/shard_map/ppermute | solution.py:10
  158.5 26.2 %collective-permute-start.11 = (f32[384,768]{1,0:T(8,128)S(1)}, f32[384,768]{1,0:T(8,128)S(1)}, u32[]{:S(2)}, u32[]{:S(2)}) collective-permute-start(f32[384,768]{1,0:T(8,128)S(1)} %collective-permute-done.9), channel_id=1, source_target_pairs={{2,0},{4,2},{6,4},{8,6},{10,8},{12,10},{14,12},{16,14},{18,16},{20... | collective-permute-start | bytes 3538952 | tf_op jit(solution)/shard_map/ppermute | solution.py:10
  179.2 25.3 %collective-permute-start.12 = (f32[768,384]{1,0:T(8,128)S(1)}, f32[768,384]{1,0:T(8,128)S(1)}, u32[]{:S(2)}, u32[]{:S(2)}) collective-permute-start(f32[768,384]{1,0:T(8,128)S(1)} %collective-permute-done.10), channel_id=1, source_target_pairs={{32,0},{64,32},{96,64},{128,96},{160,128},{192,160},{224,192},{256... | collective-permute-start | bytes 3538952 | tf_op jit(solution)/shard_map/ppermute | solution.py:10
  184.8 19.7 %collective-permute-start.13 = (f32[384,768]{1,0:T(8,128)S(1)}, f32[384,768]{1,0:T(8,128)S(1)}, u32[]{:S(2)}, u32[]{:S(2)}) collective-permute-start(f32[384,768]{1,0:T(8,128)S(1)} %collective-permute-done.11), channel_id=1, source_target_pairs={{2,0},{4,2},{6,4},{8,6},{10,8},{12,10},{14,12},{16,14},{18,16},{20... | collective-permute-start | bytes 3538952 | tf_op jit(solution)/shard_map/ppermute | solution.py:10
where the time goes:
time: 210 us; the launch traced here: 209 us
  waiting for transfers between devices  116 us (55%)
  starting transfers between devices  58.8 us (28%)
  matrix products  30.9 us (15%)
    ppermute x14, waiting for transfers between devices, passed_along(): return lax.ppermute(block, axis, route)  116 us
    ppermute x14, starting transfers between devices, passed_along(): return lax.ppermute(block, axis, route)  58.8 us
    dot_general x8, matrix products, product(): jnp.dot(lhs_block, rhs_block, preferred_element_type=jnp.float32, precisi...  30.9 us
  transfers between devices with their start and end apart: 14, of which 7 were waited for; matrix products, arithmetic and copies ran while one was open for 13% of the time, Pallas kernels for 0%

commit v1 on v0

v1 whole, which is shorter than its diff:
```python
import functools

import jax
import jax.numpy as jnp
from jax import lax
from jax.experimental import pallas as pl
from jax.experimental.pallas import tpu as pltpu
from jax.sharding import PartitionSpec as P

MESH = pl.DeviceIdType.MESH
F32, BF16 = jnp.float32, jnp.bfloat16

NZ = 16
TURNS = 8
DOWN_HOPS, UP_HOPS = TURNS - 1, NZ - 1
DOWN_ROWS = 528
DOWN_CHUNKS, UP_CHUNKS = 3, 2
TILE = 128


def split(value):
    high = value.astype(BF16)
    return high, (value - high.astype(F32)).astype(BF16)


def kernel(
    sigma_hbm, factor_hbm, mask_ref, out_ref,
    own, other, relay, factor, down, up, rhs_high, rhs_low,
    load_sem, down_send, down_recv, up_send, up_recv,
    y_send, y_recv, x_send, x_recv, pair_send, pair_recv,
):
    rows, inner = sigma_hbm.shape
    half = rows // 2
    up_rows = inner - DOWN_ROWS
    down_chunk, up_chunk = DOWN_ROWS // DOWN_CHUNKS, up_rows // UP_CHUNKS
    z, col, fr = lax.axis_index("row"), lax.axis_index("col"), lax.axis_index("fr")
    core, x, y = col % 2, (col // 2) % 4, (col // 8) * 2 + fr

    def at_z(step):
        return ((z + step + NZ) % NZ, col, fr)

    def at_x(step):
        return (z, (col // 8) * 8 + ((x + step + 4) % 4) * 2 + core, fr)

    def at_y(step):
        there = (y + step + 4) % 4
        return (z, (there // 2) * 8 + x * 2 + core, there % 2)

    sibling = (z, col + 1 - 2 * core, fr)

    sigma_load = pltpu.make_async_copy(sigma_hbm, own.at[0], load_sem.at[0])
    factor_load = pltpu.make_async_copy(factor_hbm, factor, load_sem.at[1])
    factor_load.start()
    sigma_load.start()

    barrier = pltpu.get_barrier_semaphore()
    peers = (at_z(-1), at_z(1), at_y(-1), at_y(1), at_x(1), at_x(2), at_x(3), sibling)
    for peer in peers:
        pl.semaphore_signal(barrier, inc=1, device_id=peer, device_id_type=MESH)

    def send(src, dst, send_sem, recv_sem, peer):
        return pltpu.make_async_remote_copy(
            src_ref=src, dst_ref=dst, send_sem=send_sem, recv_sem=recv_sem,
            device_id=peer, device_id_type=MESH,
        )

    def down_copy(step, piece):
        span = pl.ds(piece * down_chunk, down_chunk)
        source = factor.at[span] if step == 0 else down.at[step - 1, span]
        return send(source, down.at[step, span], down_send.at[step, piece], down_recv.at[step, piece], at_z(-1))

    def up_copy(step, piece):
        span = pl.ds(piece * up_chunk, up_chunk)
        source = factor.at[pl.ds(DOWN_ROWS + piece * up_chunk, up_chunk)] if step == 0 else up.at[step - 1, span]
        return send(source, up.at[step, span], up_send.at[step, piece], up_recv.at[step, piece], at_z(1))

    def y_copy(leg, way):
        span = pl.ds(way * half, half)
        source = own.at[0, span] if leg == 0 else relay.at[way]
        target = relay.at[way] if leg == 0 else own.at[4, span]
        return send(source, target, y_send.at[leg, way], y_recv.at[leg, way], at_y(1 - 2 * way))

    def x_copy(distance):
        which = jnp.where(x >= distance, 0, 4)
        return send(own.at[which], own.at[distance], x_send.at[distance - 1], x_recv.at[distance - 1], at_x(-distance))

    def pair_copy(distance):
        slot = distance - 1 + core
        return send(own.at[distance], other.at[slot], pair_send.at[slot], pair_recv.at[slot], sibling)

    def pair_arrival(slot):
        return send(other.at[slot], other.at[slot], pair_send.at[slot], pair_recv.at[slot], sibling)

    def multiply(turn):
        if turn == 0:
            high, low = split(factor[...])
            rhs_high[...] = high
            rhs_low[...] = low
        else:
            high, low = split(down[turn - 1])
            rhs_high[pl.ds(0, DOWN_ROWS)] = high
            rhs_low[pl.ds(0, DOWN_ROWS)] = low
            high, low = split(up[NZ - 1 - turn])
            rhs_high[pl.ds(DOWN_ROWS, up_rows)] = high
            rhs_low[pl.ds(DOWN_ROWS, up_rows)] = low

        @pl.loop(0, rows // TILE)
        def _(tile):
            span = pl.ds(pl.multiple_of(tile * TILE, TILE), TILE)
            block = own[turn // 2, span] if turn % 2 == 0 else other[turn // 2, span]
            high, low = split(block)
            dot = functools.partial(jnp.dot, preferred_element_type=F32)
            value = dot(high, rhs_high[...]) + (dot(high, rhs_low[...]) + dot(low, rhs_high[...]))
            out_ref[span] = -value if turn == 0 else out_ref[span] - value

    factor_load.wait()
    factor[...] = factor[...] * mask_ref[0, 0].astype(F32)
    sigma_load.wait()
    pl.semaphore_wait(barrier, len(peers))

    for piece in range(max(DOWN_CHUNKS, UP_CHUNKS)):
        if piece < DOWN_CHUNKS:
            down_copy(0, piece).start()
        if piece < UP_CHUNKS:
            up_copy(0, piece).start()
    for way in range(2):
        y_copy(0, way).start()
    for distance in (1, 3, 2):

        @pl.when(x >= distance)
        def _():
            x_copy(distance).start()

    @pl.when(core == 1)
    def _():
        pair_copy(0).start()

    multiply(0)

    def down_event(step, piece):
        down_copy(step, piece).wait_recv()
        if step + 1 < DOWN_HOPS:
            down_copy(step + 1, piece).start()

    def up_event(step, piece):
        up_copy(step, piece).wait_recv()
        if step + 1 < UP_HOPS:
            up_copy(step + 1, piece).start()

    def y_event(leg):
        for way in range(2):
            y_copy(leg, way).wait_recv()
            if leg == 0:
                y_copy(1, way).start()
        if leg == 1:
            for distance in (1, 3, 2):

                @pl.when(x < distance)
                def _():
                    x_copy(distance).start()

            @pl.when(core == 0)
            def _():
                pair_copy(4).start()

    def x_event(distance):
        x_copy(distance).wait_recv()
        pair_copy(distance).start()

    def pair_event():
        for slot in range(4):
            pair_arrival(slot).wait_recv()

    events = [
        (0.14, functools.partial(y_event, 0)),
        (0.28, functools.partial(y_event, 1)),
        (0.55, functools.partial(x_event, 1)),
        (0.56, functools.partial(x_event, 3)),
        (0.72, functools.partial(x_event, 2)),
        (0.745, pair_event),
    ]
    for step in range(DOWN_HOPS):
        for piece in range(DOWN_CHUNKS):
            events.append(((step + (piece + 1) / DOWN_CHUNKS) / DOWN_HOPS, functools.partial(down_event, step, piece)))
    for step in range(UP_HOPS):
        for piece in range(UP_CHUNKS):
            events.append(((step + (piece + 1) / UP_CHUNKS) / UP_HOPS, functools.partial(up_event, step, piece)))
    for turn in range(1, TURNS):
        ready = max(turn / DOWN_HOPS, (NZ - turn) / UP_HOPS)
        events.append((max(ready, 0.75) + 0.001, functools.partial(multiply, turn)))
    for _, event in sorted(events, key=lambda entry: entry[0]):
        event()

    for step in range(DOWN_HOPS):
        for piece in range(DOWN_CHUNKS):
            down_copy(step, piece).wait_send()
    for step in range(UP_HOPS):
        for piece in range(UP_CHUNKS):
            up_copy(step, piece).wait_send()
    for leg in range(2):
        for way in range(2):
            y_copy(leg, way).wait_send()
    for distance in (1, 2, 3):
        x_copy(distance).wait_send()
    for slot in range(4):
        pair_arrival(slot).wait_send()


def body(sigma_aa, l_as, block_mask):
    rows, inner = sigma_aa.shape
    width = l_as.shape[1]
    up_rows = inner - DOWN_ROWS
    dma = pltpu.SemaphoreType.DMA
    return pl.pallas_call(
        kernel,
        out_shape=jax.ShapeDtypeStruct((rows, width), F32),
        in_specs=[
            pl.BlockSpec(memory_space=pl.ANY),
            pl.BlockSpec(memory_space=pl.ANY),
            pl.BlockSpec(memory_space=pltpu.SMEM),
        ],
        out_specs=pl.BlockSpec(memory_space=pltpu.VMEM),
        scratch_shapes=[
            pltpu.VMEM((5, rows, inner), F32),
            pltpu.VMEM((4, rows, inner), F32),
            pltpu.VMEM((2, rows // 2, inner), F32),
            pltpu.VMEM((inner, width), F32),
            pltpu.VMEM((DOWN_HOPS, DOWN_ROWS, width), F32),
            pltpu.VMEM((UP_HOPS, up_rows, width), F32),
            pltpu.VMEM((inner, width), BF16),
            pltpu.VMEM((inner, width), BF16),
            dma((2,)),
            dma((DOWN_HOPS, DOWN_CHUNKS)),
            dma((DOWN_HOPS, DOWN_CHUNKS)),
            dma((UP_HOPS, UP_CHUNKS)),
            dma((UP_HOPS, UP_CHUNKS)),
            dma((2, 2)),
            dma((2, 2)),
            dma((3,)),
            dma((3,)),
            dma((4,)),
            dma((4,)),
        ],
        compiler_params=pltpu.CompilerParams(
            collective_id=0, has_side_effects=True, vmem_limit_bytes=56 << 20
        ),
        name="front_product",
    )(sigma_aa, l_as, block_mask)


def solution(mesh):
    placed = (P(("fr", "row"), "col"), P(("fr", "row"), "col"), P(("fr", "row"), "col"))
    return jax.shard_map(
        body, mesh=mesh, in_specs=placed, out_specs=P(("fr", "row"), "col"), check_vma=False
    )
```

time: 210 us -> 153 us (0.73)
  Pallas kernels: 0 us -> 150 us
  waiting for transfers between devices: 116 us -> 0 us
  starting transfers between devices: 58.8 us -> 0 us
  matrix products: 30.9 us -> 0 us
    pallas_call x0 -> x1, Pallas kernels: none -> 150 us  [body(): pl.pallas_call(kernel, out_shape=jax.ShapeDtypeStruct((rows, width), F32)...]
    ppermute x14 -> x0, waiting for transfers between devices: 116 us -> none  [passed_along(): return lax.ppermute(block, axis, route)]
    ppermute x14 -> x0, starting transfers between devices: 58.8 us -> none  [passed_along(): return lax.ppermute(block, axis, route)]
    dot_general x8 -> x0, matrix products: 30.9 us -> none  [product(): jnp.dot(lhs_block, rhs_block, preferred_element_type=jnp.float32, precisi...]
  transfers between devices with their start and end apart: 14 -> 0, of which waited for: 7 -> 0; matrix products, arithmetic and copies ran while one was open for 13% -> 0% of each run, Pallas kernels for 0% -> 0%
where the time goes in v1:
time: 153 us; the launch traced here: 152 us
  Pallas kernels  150 us (98%)
  local copies, waits for them, and re-layouts  1.92 us (1%)
    pallas_call x1, Pallas kernels, body(): pl.pallas_call(kernel, out_shape=jax.ShapeDtypeStruct((rows, width), F32)...  150 us

profile of v1, /device:TPU:6, one launch (start us, length us, event | category | flops | bytes accessed | tf_op | source)
XLA Modules:
  0.0 152.2 jit_solution(18415308111633496058)
XLA Ops:
  0.7 149.6 %front_product.1 = f32[384,384]{1,0:T(8,128)} custom-call(f32[384,768]{1,0:T(8,128)} %sigma_hbm.1, f32[768,384]{1,0:T(8,128)} %factor_hbm.1, s32[1,1]{1,0:T(1,128)S(6)} %copy.5.mask_ref), custom_call_target="tpu_custom_call" | custom-call | tf_op jit(solution)/shard_map/front_product/pallas_call | solution.py:214
  150.3 1.9 %copy.6 = f32[384,384]{1,0:T(8,128)} copy(f32[384,384]{1,0:T(8,128)} %front_product.1) | data formatting | bytes 1179648

commit v2 on v1

--- a/solution.py
+++ b/solution.py
@@ -16,6 +16,7 @@
 DOWN_ROWS = 528
 DOWN_CHUNKS, UP_CHUNKS = 3, 2
 TILE = 128
+AT_Y, AT_X, AT_PAIR = (0.14, 0.28), (0.8, 0.805, 0.81), 0.83
 
 
 def split(value):
@@ -65,7 +66,7 @@
         )
 
     def down_copy(step, piece):
-        span = pl.ds(piece * down_chunk, down_chunk)
+        span = pl.ds((DOWN_CHUNKS - 1 - piece) * down_chunk, down_chunk)
         source = factor.at[span] if step == 0 else down.at[step - 1, span]
         return send(source, down.at[step, span], down_send.at[step, piece], down_recv.at[step, piece], at_z(-1))
 
@@ -91,26 +92,30 @@
     def pair_arrival(slot):
         return send(other.at[slot], other.at[slot], pair_send.at[slot], pair_recv.at[slot], sibling)
 
-    def multiply(turn):
+    def multiply(turn, low_row=0, high_row=None):
+        high_row = inner if high_row is None else high_row
+        depth, middle = high_row - low_row, min(max(low_row, DOWN_ROWS), high_row)
+
+        def take(source, start, stop, target):
+            if stop > start:
+                high, low = split(source[pl.ds(start, stop - start)])
+                rhs_high[pl.ds(target, stop - start)] = high
+                rhs_low[pl.ds(target, stop - start)] = low
+
         if turn == 0:
-            high, low = split(factor[...])
-            rhs_high[...] = high
-            rhs_low[...] = low
+            take(factor, low_row, high_row, 0)
         else:
-            high, low = split(down[turn - 1])
-            rhs_high[pl.ds(0, DOWN_ROWS)] = high
-            rhs_low[pl.ds(0, DOWN_ROWS)] = low
-            high, low = split(up[NZ - 1 - turn])
-            rhs_high[pl.ds(DOWN_ROWS, up_rows)] = high
-            rhs_low[pl.ds(DOWN_ROWS, up_rows)] = low
+            take(down.at[turn - 1], low_row, middle, 0)
+            take(up.at[NZ - 1 - turn], middle - DOWN_ROWS, high_row - DOWN_ROWS, middle - low_row)
 
         @pl.loop(0, rows // TILE)
         def _(tile):
             span = pl.ds(pl.multiple_of(tile * TILE, TILE), TILE)
-            block = own[turn // 2, span] if turn % 2 == 0 else other[turn // 2, span]
-            high, low = split(block)
+            lhs = own if turn % 2 == 0 else other
+            high, low = split(lhs[turn // 2, span, pl.ds(low_row, depth)])
             dot = functools.partial(jnp.dot, preferred_element_type=F32)
-            value = dot(high, rhs_high[...]) + (dot(high, rhs_low[...]) + dot(low, rhs_high[...]))
+            one, two = rhs_high[pl.ds(0, depth)], rhs_low[pl.ds(0, depth)]
+            value = dot(high, one) + (dot(high, two) + dot(low, one))
             out_ref[span] = -value if turn == 0 else out_ref[span] - value
 
     factor_load.wait()
@@ -171,23 +176,24 @@
         for slot in range(4):
             pair_arrival(slot).wait_recv()
 
-    events = [
-        (0.14, functools.partial(y_event, 0)),
-        (0.28, functools.partial(y_event, 1)),
-        (0.55, functools.partial(x_event, 1)),
-        (0.56, functools.partial(x_event, 3)),
-        (0.72, functools.partial(x_event, 2)),
-        (0.745, pair_event),
-    ]
+    whole = DOWN_ROWS * DOWN_HOPS
+    events = [(AT_Y[leg], functools.partial(y_event, leg)) for leg in range(2)]
+    events += [(when, functools.partial(x_event, distance)) for when, distance in zip(AT_X, (1, 3, 2))]
+    events += [(AT_PAIR, pair_event)]
     for step in range(DOWN_HOPS):
         for piece in range(DOWN_CHUNKS):
-            events.append(((step + (piece + 1) / DOWN_CHUNKS) / DOWN_HOPS, functools.partial(down_event, step, piece)))
+            when = (step * DOWN_ROWS + (piece + 1) * down_chunk) / whole
+            events.append((when, functools.partial(down_event, step, piece)))
     for step in range(UP_HOPS):
         for piece in range(UP_CHUNKS):
-            events.append(((step + (piece + 1) / UP_CHUNKS) / UP_HOPS, functools.partial(up_event, step, piece)))
-    for turn in range(1, TURNS):
-        ready = max(turn / DOWN_HOPS, (NZ - turn) / UP_HOPS)
-        events.append((max(ready, 0.75) + 0.001, functools.partial(multiply, turn)))
+            when = (step * up_rows + (piece + 1) * up_chunk) / whole
+            events.append((when, functools.partial(up_event, step, piece)))
+    last_up = up_rows * UP_HOPS / whole
+    products = [(last_up * 0.99, 1, 0, 512), (last_up, 1, 512, inner), (1 - 1 / (DOWN_CHUNKS * DOWN_HOPS), 7, 256, inner), (1, 7, 0, 256)]
+    for turn in range(2, TURNS - 1):
+        products.append((max(turn * DOWN_ROWS, (NZ - turn) * up_rows) / whole, turn, 0, inner))
+    for when, *product in products:
+        events.append((max(when, AT_PAIR) + 1e-4, functools.partial(multiply, *product)))
     for _, event in sorted(events, key=lambda entry: entry[0]):
         event()
 
@@ -215,8 +221,8 @@
         kernel,
         out_shape=jax.ShapeDtypeStruct((rows, width), F32),
         in_specs=[
-            pl.BlockSpec(memory_space=pl.ANY),
-            pl.BlockSpec(memory_space=pl.ANY),
+            pl.BlockSpec(memory_space=pltpu.HBM),
+            pl.BlockSpec(memory_space=pltpu.HBM),
             pl.BlockSpec(memory_space=pltpu.SMEM),
         ],
         out_specs=pl.BlockSpec(memory_space=pltpu.VMEM),
@@ -242,7 +248,7 @@
             dma((4,)),
         ],
         compiler_params=pltpu.CompilerParams(
-            collective_id=0, has_side_effects=True, vmem_limit_bytes=56 << 20
+            collective_id=0, has_side_effects=True, vmem_limit_bytes=53 << 20
         ),
         name="front_product",
     )(sigma_aa, l_as, block_mask)

time: 153 us -> 138 us (0.902)
  Pallas kernels: 150 us -> 135 us
    pallas_call x1, Pallas kernels: 150 us -> 135 us  [body(): pl.pallas_call(kernel, out_shape=jax.ShapeDtypeStruct((rows, width), F32)...]
where the time goes in v2:
time: 138 us; the launch traced here: 136 us
  Pallas kernels  135 us (98%)
    pallas_call x1, Pallas kernels, body(): pl.pallas_call(kernel, out_shape=jax.ShapeDtypeStruct((rows, width), F32)...  135 us

profile of v2, /device:TPU:6, one launch (start us, length us, event | category | flops | bytes accessed | tf_op | source)
XLA Modules:
  0.0 136.0 jit_solution(11800574307717498437)
XLA Ops:
  0.7 134.5 %front_product.1 = f32[384,384]{1,0:T(8,128)S(1)} custom-call(f32[384,768]{1,0:T(8,128)} %sigma_hbm.1, f32[768,384]{1,0:T(8,128)} %factor_hbm.1, s32[1,1]{1,0:T(1,128)S(6)} %copy.5.mask_ref), custom_call_target="tpu_custom_call" | custom-call | tf_op jit(solution)/shard_map/front_product/pallas_call | solution.py:220
  135.2 0.8 copy.6

commit v3 on v2

v3 whole, which is shorter than its diff:
```python
import functools

import jax
import jax.numpy as jnp
from jax import lax
from jax.experimental import pallas as pl
from jax.experimental.pallas import tpu as pltpu
from jax.sharding import PartitionSpec as P

MESH = pl.DeviceIdType.MESH
F32, BF16 = jnp.float32, jnp.bfloat16

NZ = 16
TURNS = 8
DOWN_HOPS, UP_HOPS = TURNS - 1, NZ - 1
DOWN_PIECES = (
    (384, 104, True), (488, 104, True), (288, 96, False), (192, 96, False), (96, 96, False), (0, 96, False),
)
UP_PIECES = (
    (384, 104, True), (488, 104, True), (592, 48, False), (640, 48, False), (688, 40, False), (728, 40, False),
)
CLIMB_SHARE = 5 / 16
DOWN_LATE = 120
TILE_GAP = 25
TILE = 128
AT_Y, AT_X, AT_PAIR = (0.14, 0.28), (0.75, 0.755, 0.76), 0.78


def climbs(block):
    return ((block < 5) & (block % 2 == 0)) | (block == 9) | (block == 11)


def split(value):
    high = value.astype(BF16)
    return high, (value - high.astype(F32)).astype(BF16)


def kernel(
    sigma_hbm, factor_hbm, mask_ref, out_ref,
    own, other, relay, factor, blocks, passing, rhs_high, rhs_low,
    load_sem, below_sem, peer_sem, down_send, down_recv, up_send, up_recv,
    y_send, y_recv, x_send, x_recv, pair_send, pair_recv,
):
    rows, inner = sigma_hbm.shape
    half = rows // 2
    z, col, fr = lax.axis_index("row"), lax.axis_index("col"), lax.axis_index("fr")
    core, x, y = col % 2, (col // 2) % 4, (col // 8) * 2 + fr

    def at_z(step):
        return ((z + step + NZ) % NZ, col, fr)

    def at_x(step):
        return (z, (col // 8) * 8 + ((x + step + 4) % 4) * 2 + core, fr)

    def at_y(step):
        there = (y + step + 4) % 4
        return (z, (there // 2) * 8 + x * 2 + core, there % 2)

    sibling = (z, col + 1 - 2 * core, fr)

    sigma_load = pltpu.make_async_copy(sigma_hbm, own.at[0], load_sem.at[0])
    factor_load = pltpu.make_async_copy(factor_hbm, factor, load_sem.at[1])
    factor_load.start()
    sigma_load.start()

    def entry(where):
        _, there, group = where
        place = (((there // 8) * 2 + group) * 4 + (there // 2) % 4) * 2 + there % 2
        return jnp.where((z == 0) & (place == 0), NZ * NZ, place)

    mine = entry((z, col, fr))
    peers = [(peer, entry(peer)) for peer in (at_y(-1), at_y(1), at_x(1), at_x(2), at_x(3), sibling)]
    earlier = sum((place < mine).astype(jnp.int32) for _, place in peers)

    def tell(semaphore, peer):
        pl.semaphore_signal(semaphore, inc=1, device_id=peer, device_id_type=MESH)

    barrier = pltpu.get_barrier_semaphore()
    tell(barrier, at_z(-1))
    for peer, place in peers:
        pl.when(place > mine)(functools.partial(tell, barrier, peer))

    def send(src, dst, send_sem, recv_sem, peer):
        return pltpu.make_async_remote_copy(
            src_ref=src, dst_ref=dst, send_sem=send_sem, recv_sem=recv_sem,
            device_id=peer, device_id_type=MESH,
        )

    def down_copy(step, piece):
        first, count, _ = DOWN_PIECES[piece]
        span = pl.ds(first, count)
        source = factor if step == 0 else blocks.at[step]
        return send(
            source.at[span], blocks.at[step + 1, span],
            down_send.at[step, piece], down_recv.at[step, piece], at_z(-1),
        )

    def climbed(step, span):
        if step <= UP_HOPS - TURNS:
            return passing.at[step, pl.ds(span.start - UP_PIECES[0][0], span.size)]
        return blocks.at[UP_HOPS - step, span]

    def up_copy(step, piece):
        first, count, _ = UP_PIECES[piece]
        span = pl.ds(first, count)
        source = factor.at[span] if step == 0 else climbed(step - 1, span)
        return send(
            source, climbed(step, span),
            up_send.at[step, piece], up_recv.at[step, piece], at_z(1),
        )

    def only_if(needed, condition, action):
        if needed:
            pl.when(condition)(action)
        else:
            action()

    def down_do(block_step, piece, action):
        only_if(DOWN_PIECES[piece][2], jnp.logical_not(climbs((z + block_step) % NZ)), action)

    def up_do(block_step, piece, action):
        only_if(UP_PIECES[piece][2], climbs((z + NZ - block_step) % NZ), action)

    def y_copy(leg, way):
        span = pl.ds(way * half, half)
        source = own.at[0, span] if leg == 0 else relay.at[way]
        target = relay.at[way] if leg == 0 else own.at[4, span]
        return send(source, target, y_send.at[leg, way], y_recv.at[leg, way], at_y(1 - 2 * way))

    def x_copy(distance):
        which = jnp.where(x >= distance, 0, 4)
        return send(own.at[which], own.at[distance], x_send.at[distance - 1], x_recv.at[distance - 1], at_x(-distance))

    def pair_copy(distance):
        slot = distance - 1 + core
        return send(own.at[distance], other.at[slot], pair_send.at[slot], pair_recv.at[slot], sibling)

    def pair_arrival(slot):
        return send(other.at[slot], other.at[slot], pair_send.at[slot], pair_recv.at[slot], sibling)

    def multiply(tile, turn, low_row=0, high_row=None):
        high_row = inner if high_row is None else high_row
        depth = high_row - low_row
        if tile == 0:
            source = factor if turn == 0 else blocks.at[turn]
            high, low = split(source[pl.ds(low_row, depth)])
            rhs_high[pl.ds(0, depth)] = high
            rhs_low[pl.ds(0, depth)] = low
        span = pl.ds(tile * TILE, TILE)
        lhs = own if turn % 2 == 0 else other
        high, low = split(lhs[turn // 2, span, pl.ds(low_row, depth)])
        dot = functools.partial(jnp.dot, preferred_element_type=F32)
        one, two = rhs_high[pl.ds(0, depth)], rhs_low[pl.ds(0, depth)]
        value = dot(high, one) + (dot(high, two) + dot(low, one))
        out_ref[span] = -value if turn == 0 else out_ref[span] - value

    factor_load.wait()
    factor[...] = factor[...] * mask_ref[0, 0].astype(F32)
    sigma_load.wait()
    pl.semaphore_wait(barrier, 1 + earlier)
    tell(below_sem, at_z(1))
    for piece in range(len(UP_PIECES)):
        up_do(0, piece, up_copy(0, piece).start)
    for peer, place in peers:
        pl.when(place < mine)(functools.partial(tell, peer_sem, peer))
    pl.semaphore_wait(below_sem, 1)
    for piece in range(len(DOWN_PIECES)):
        down_do(0, piece, down_copy(0, piece).start)

    @pl.when(earlier < len(peers))
    def _():
        pl.semaphore_wait(peer_sem, len(peers) - earlier)

    for way in range(2):
        y_copy(0, way).start()
    for distance in (1, 3, 2):

        @pl.when(x >= distance)
        def _():
            x_copy(distance).start()

    @pl.when(core == 1)
    def _():
        pair_copy(0).start()

    for tile in range(rows // TILE):
        multiply(tile, 0)

    def down_event(step, piece):
        def action():
            down_copy(step, piece).wait_recv()
            if step + 1 < DOWN_HOPS:
                down_copy(step + 1, piece).start()

        down_do(step + 1, piece, action)

    def up_event(step, piece):
        def action():
            up_copy(step, piece).wait_recv()
            if step + 1 < UP_HOPS:
                up_copy(step + 1, piece).start()

        up_do(step + 1, piece, action)

    def y_event(leg):
        for way in range(2):
            y_copy(leg, way).wait_recv()
            if leg == 0:
                y_copy(1, way).start()
        if leg == 1:
            for distance in (1, 3, 2):

                @pl.when(x < distance)
                def _():
                    x_copy(distance).start()

            @pl.when(core == 0)
            def _():
                pair_copy(4).start()

    def x_event(distance):
        x_copy(distance).wait_recv()
        pair_copy(distance).start()

    def pair_event():
        for slot in range(4):
            pair_arrival(slot).wait_recv()

    def arrivals(pieces, share, hops):
        sizes = [count * (share if either else 1) for _, count, either in pieces]
        return [[step * sum(sizes) + sum(sizes[: piece + 1]) for piece in range(len(sizes))] for step in range(hops)]

    down_times = arrivals(DOWN_PIECES, 1 - CLIMB_SHARE, DOWN_HOPS)
    up_times = arrivals(UP_PIECES, CLIMB_SHARE, UP_HOPS)
    whole = max(down_times[-1][-1], up_times[-1][-1])
    events = [(AT_Y[leg] * whole, functools.partial(y_event, leg)) for leg in range(2)]
    events += [(when * whole, functools.partial(x_event, distance)) for when, distance in zip(AT_X, (1, 3, 2))]
    events += [(AT_PAIR * whole, pair_event)]
    down_times = [[min(when + DOWN_LATE, max(when, whole - 0.1 * (len(row) - 1 - piece))) for piece, when in enumerate(row)] for row in down_times]
    for times, event in ((down_times, down_event), (up_times, up_event)):
        for step, row in enumerate(times):
            for piece, when in enumerate(row):
                events.append((when, functools.partial(event, step, piece)))
    products = [
        (up_times[-1][1], 1, 0, 512), (up_times[-1][-1], 1, 512, inner),
        (down_times[-1][3], TURNS - 1, 256, inner), (down_times[-1][-1], TURNS - 1, 0, 256),
    ]
    for turn in range(2, TURNS - 1):
        products.append((max(down_times[turn - 1][-1], up_times[UP_HOPS - turn][-1]), turn, 0, inner))
    free = AT_PAIR * whole
    for when, *product in sorted(products):
        for tile in range(rows // TILE):
            free = max(when, free) + 0.01
            events.append((free, functools.partial(multiply, tile, *product)))
            free += TILE_GAP
    for _, event in sorted(events, key=lambda entry: entry[0]):
        event()

    for step in range(DOWN_HOPS):
        for piece in range(len(DOWN_PIECES)):
            down_do(step, piece, down_copy(step, piece).wait_send)
    for step in range(UP_HOPS):
        for piece in range(len(UP_PIECES)):
            up_do(step, piece, up_copy(step, piece).wait_send)
    for leg in range(2):
        for way in range(2):
            y_copy(leg, way).wait_send()
    for distance in (1, 2, 3):
        x_copy(distance).wait_send()
    for slot in range(4):
        pair_arrival(slot).wait_send()


def body(sigma_aa, l_as, block_mask):
    rows, inner = sigma_aa.shape
    width = l_as.shape[1]
    dma = pltpu.SemaphoreType.DMA
    return pl.pallas_call(
        kernel,
        out_shape=jax.ShapeDtypeStruct((rows, width), F32),
        in_specs=[
            pl.BlockSpec(memory_space=pltpu.HBM),
            pl.BlockSpec(memory_space=pltpu.HBM),
            pl.BlockSpec(memory_space=pltpu.SMEM),
        ],
        out_specs=pl.BlockSpec(memory_space=pltpu.VMEM),
        scratch_shapes=[
            pltpu.VMEM((5, rows, inner), F32),
            pltpu.VMEM((4, rows, inner), F32),
            pltpu.VMEM((2, rows // 2, inner), F32),
            pltpu.VMEM((inner, width), F32),
            pltpu.VMEM((TURNS, inner, width), F32),
            pltpu.VMEM((UP_HOPS - TURNS + 1, inner - UP_PIECES[0][0], width), F32),
            pltpu.VMEM((inner, width), BF16),
            pltpu.VMEM((inner, width), BF16),
            dma((2,)),
            pltpu.SemaphoreType.REGULAR,
            pltpu.SemaphoreType.REGULAR,
            dma((DOWN_HOPS, len(DOWN_PIECES))),
            dma((DOWN_HOPS, len(DOWN_PIECES))),
            dma((UP_HOPS, len(UP_PIECES))),
            dma((UP_HOPS, len(UP_PIECES))),
            dma((2, 2)),
            dma((2, 2)),
            dma((3,)),
            dma((3,)),
            dma((4,)),
            dma((4,)),
        ],
        compiler_params=pltpu.CompilerParams(
            collective_id=0, has_side_effects=True, vmem_limit_bytes=53 << 20
        ),
        name="front_product",
    )(sigma_aa, l_as, block_mask)


def solution(mesh):
    placed = (P(("fr", "row"), "col"), P(("fr", "row"), "col"), P(("fr", "row"), "col"))
    return jax.shard_map(
        body, mesh=mesh, in_specs=placed, out_specs=P(("fr", "row"), "col"), check_vma=False
    )
```

time: 138 us -> 136 us (0.986)
  Pallas kernels: 135 us -> 132 us
    pallas_call x1, Pallas kernels: 135 us -> 132 us  [body(): pl.pallas_call(kernel, out_shape=jax.ShapeDtypeStruct((rows, width), F32)...]
where the time goes in v3:
time: 136 us; the launch traced here: 133 us
  Pallas kernels  132 us (97%)
    pallas_call x1, Pallas kernels, body(): pl.pallas_call(kernel, out_shape=jax.ShapeDtypeStruct((rows, width), F32)...  132 us

profile of v3, /device:TPU:6, one launch (start us, length us, event | category | flops | bytes accessed | tf_op | source)
XLA Modules:
  0.0 133.2 jit_solution(134520714432923455)
XLA Ops:
  0.7 131.7 %front_product.1 = f32[384,384]{1,0:T(8,128)S(1)} custom-call(f32[384,768]{1,0:T(8,128)} %sigma_hbm.1, f32[768,384]{1,0:T(8,128)} %factor_hbm.1, s32[1,1]{1,0:T(1,128)S(6)} %copy.5.mask_ref), custom_call_target="tpu_custom_call" | custom-call | tf_op jit(solution)/shard_map/front_product/pallas_call | solution.py:278
  132.4 0.8 copy.6

commit v4 on v3

--- a/solution.py
+++ b/solution.py
@@ -14,20 +14,19 @@
 TURNS = 8
 DOWN_HOPS, UP_HOPS = TURNS - 1, NZ - 1
 DOWN_PIECES = (
-    (384, 104, True), (488, 104, True), (288, 96, False), (192, 96, False), (96, 96, False), (0, 96, False),
+    (440, 80, True), (520, 80, True), (328, 112, False), (216, 112, False), (112, 104, False), (0, 112, False),
 )
-UP_PIECES = (
-    (384, 104, True), (488, 104, True), (592, 48, False), (640, 48, False), (688, 40, False), (728, 40, False),
-)
-CLIMB_SHARE = 5 / 16
-DOWN_LATE = 120
+UP_PIECES = ((440, 80, True), (520, 80, True), (600, 56, False), (656, 56, False), (712, 56, False))
+CLIMB_SHARE = 7 / 16
+DOWN_LATE = 60
 TILE_GAP = 25
 TILE = 128
 AT_Y, AT_X, AT_PAIR = (0.14, 0.28), (0.75, 0.755, 0.76), 0.78
 
 
 def climbs(block):
-    return ((block < 5) & (block % 2 == 0)) | (block == 9) | (block == 11)
+    even = block % 2 == 0
+    return ((block < 7) & even) | ((block > 8) & (block < 14) & jnp.logical_not(even))
 
 
 def split(value):

time: 136 us -> 134 us (0.985); the launches traced: 133 us -> 133 us
  no operation moved by 1% of the time
where the time goes in v4:
time: 134 us; the launch traced here: 133 us
  Pallas kernels  131 us (98%)
    pallas_call x1, Pallas kernels, body(): pl.pallas_call(kernel, out_shape=jax.ShapeDtypeStruct((rows, width), F32)...  131 us

profile of v4, /device:TPU:6, one launch (start us, length us, event | category | flops | bytes accessed | tf_op | source)
XLA Modules:
  0.0 132.9 jit_solution(11911557895442836060)
XLA Ops:
  0.7 131.4 %front_product.1 = f32[384,384]{1,0:T(8,128)S(1)} custom-call(f32[384,768]{1,0:T(8,128)} %sigma_hbm.1, f32[768,384]{1,0:T(8,128)} %factor_hbm.1, s32[1,1]{1,0:T(1,128)S(6)} %copy.5.mask_ref), custom_call_target="tpu_custom_call" | custom-call | tf_op jit(solution)/shard_map/front_product/pallas_call | solution.py:277
  132.0 0.8 copy.6

commit v5 on v4

--- a/solution.py
+++ b/solution.py
@@ -18,8 +18,8 @@
 )
 UP_PIECES = ((440, 80, True), (520, 80, True), (600, 56, False), (656, 56, False), (712, 56, False))
 CLIMB_SHARE = 7 / 16
-DOWN_LATE = 60
-TILE_GAP = 25
+DOWN_LATE = 90
+TILE_GAP = 10
 TILE = 128
 AT_Y, AT_X, AT_PAIR = (0.14, 0.28), (0.75, 0.755, 0.76), 0.78
 

time: 134 us -> 134 us (level)
  no operation moved by 1% of the time
where the time goes in v5:
time: 134 us; the launch traced here: 133 us
  Pallas kernels  131 us (98%)
    pallas_call x1, Pallas kernels, body(): pl.pallas_call(kernel, out_shape=jax.ShapeDtypeStruct((rows, width), F32)...  131 us

profile of v5, /device:TPU:6, one launch (start us, length us, event | category | flops | bytes accessed | tf_op | source)
XLA Modules:
  0.0 132.9 jit_solution(2613525572331495803)
XLA Ops:
  0.7 131.4 %front_product.1 = f32[384,384]{1,0:T(8,128)S(1)} custom-call(f32[384,768]{1,0:T(8,128)} %sigma_hbm.1, f32[768,384]{1,0:T(8,128)} %factor_hbm.1, s32[1,1]{1,0:T(1,128)S(6)} %copy.5.mask_ref), custom_call_target="tpu_custom_call" | custom-call | tf_op jit(solution)/shard_map/front_product/pallas_call | solution.py:277
  132.0 0.8 copy.6
